TPU v7x, 32 devices: a whole 2x2x4 slice. The times are simulated.
32 devices in a mesh: groups: 2 (over x), stem: 8 (over z, y), cuts: 2 (over core).
Axes of the slice: x: 2, y: 2, z: 4, core: 2. Of those that a mesh axis runs over, the one named last changes fastest.
Arguments:
- stem: bfloat16 [4, 2, 4096, 1024], P(('groups', 'cuts'), None, 'stem'), parts along dimension 0, may hold values from -6 to 6
- edge_values: int32 [4, 4], P(('groups', 'cuts')), parts along dimension 0, may hold values from 0 to 1
- index_order: int32 [1024], replicated, may hold values from 0 to 1023, each once
- branch_first: bfloat16 [2, 1024, 1024], replicated, may hold values from -0.125 to 0.125
- branch_second: bfloat16 [2, 1024, 1024], replicated, may hold values from -0.125 to 0.125
- branch_third: bfloat16 [2, 1024, 256], replicated, may hold values from -0.125 to 0.125
- edge_table: float32 [16, 2, 256], replicated, may hold values from -6 to 6
- picks: int32 [4096], P('stem'), may hold values from 0 to 511, as said below
Outputs:
- amplitudes: float32 [2, 8192, 256], P(None, ('groups', 'stem')), parts along dimension 1
There are 2 independent parts, one for each index of `groups`. A program takes and returns all parts, laid end to end along the dimension named above; an argument that names none is the same for every part. Nothing has to cross between parts.
Inputs may be any that keep to these rules, and one draw needn't show every extreme that they name: `index_order`: each number of 0 to 1023 once. `picks`: each aligned block of 512 entries names every number of 0 to 511 once.
All inputs are finite; a program needn't handle non-finite values.
Results may differ from a plain program's by a relative error of at most 0.0041.
Values may be sent and summed in bfloat16 or wider, within the bound.
No kernel may reach another device: no remote copies, remote signals or barrier semaphores. Data moves between devices by JAX's collectives and lax.ppermute only.
A program may use at most 64 MiB of HBM per device.

v0:
```python
import jax
import jax.numpy as jnp
from jax import lax
from jax.sharding import PartitionSpec as P


def swapped(value, axis, distance):
    mask = 2**distance
    pairs = [(source, source ^ mask) for source in range(lax.axis_size(axis))]
    return lax.ppermute(value, axis, pairs)


def complex_dot(operand, matrix):
    real = jnp.dot(operand[0], matrix[0], preferred_element_type=jnp.float32) - jnp.dot(
        operand[1], matrix[1], preferred_element_type=jnp.float32
    )
    imag = jnp.dot(operand[0], matrix[1], preferred_element_type=jnp.float32) + jnp.dot(
        operand[1], matrix[0], preferred_element_type=jnp.float32
    )
    return jnp.stack([real, imag])


def on_device(
    stem, edge_values, index_order, branch_first, branch_second, branch_third, edge_table, picks
):
    stem_size = lax.axis_size("stem")
    bit_pos = stem_size.bit_length() - 2
    top_bit = lax.axis_index("stem") // (stem_size // 2) % 2
    is_low = top_bit == 0
    width = branch_first.shape[1]
    half_width = width // 2
    rows_dev = stem.shape[2]
    block_rows = rows_dev // stem_size
    inverse = jnp.zeros_like(index_order).at[index_order].set(jnp.arange(width, dtype=jnp.int32))
    reordered = jnp.take(branch_second, inverse, axis=1)
    powers = 2 ** jnp.arange(edge_values.shape[1], dtype=jnp.int32)
    codes = jnp.arange(edge_table.shape[0], dtype=jnp.int32)
    first = complex_dot(stem[0], branch_first).astype(jnp.bfloat16)
    low_half = first[:, :, :half_width]
    high_half = first[:, :, half_width:]
    outgoing = jnp.where(is_low, high_half, low_half)
    incoming = swapped(outgoing, "stem", bit_pos)
    joined = jnp.where(
        is_low,
        jnp.concatenate([low_half, incoming], axis=2),
        jnp.concatenate([incoming, high_half], axis=2),
    )
    second = complex_dot(joined, reordered).astype(jnp.bfloat16)
    contracted = complex_dot(second, branch_third)
    moved = lax.all_to_all(
        contracted.reshape(2, stem_size, block_rows, contracted.shape[2]),
        "stem",
        split_axis=1,
        concat_axis=1,
        tiled=True,
    )
    third = jnp.take(moved.reshape(2, rows_dev, contracted.shape[2]), picks, axis=1)
    code = jnp.sum(edge_values[0] * powers)
    onehot = (codes == code).astype(jnp.float32)
    factor = jnp.sum(onehot[:, None, None] * edge_table, axis=0)
    real = third[0] * factor[0][None, :] - third[1] * factor[1][None, :]
    imag = third[0] * factor[1][None, :] + third[1] * factor[0][None, :]
    total = jnp.stack([real, imag])
    return lax.psum(total, "cuts")


def solution(mesh):
    return jax.shard_map(
        on_device,
        mesh=mesh,
        in_specs=(
            P(("groups", "cuts"), None, "stem", None),
            P(("groups", "cuts"), None),
            P(),
            P(),
            P(),
            P(),
            P(),
            P("stem"),
        ),
        out_specs=P(None, ("groups", "stem"), None),
        check_vma=False,
    )
```

profile of v0, /device:TPU:0, one launch (start us, length us, event | category | flops | bytes accessed | tf_op | source)
XLA Modules:
  0.0 144.1 jit_solution(4913342444032320021)
XLA Ops:
  6.5 4.6 %fusion.2 = f32[512,1024]{1,0:T(8,128)} fusion(bf16[2,1024,1024]{2,1,0:T(8,128)(2,1)} %param.11, bf16[1,2,512,1024]{3,2,1,0:T(8,128)(2,1)} %param.8), kind=kOutput, calls=%fused_computation.11 | convolution fusion | flops 1073741824 | bytes 5242880 | tf_op jit(solution)/shard_map/dot_general | solution.py:14
  11.2 0.0 copy-done.4
  11.2 0.0 copy-done.6
  11.2 2.6 %fusion = f32[512,1024]{1,0:T(8,128)} fusion(bf16[2,1024,1024]{2,1,0:T(8,128)(2,1)S(1)} %copy-done.4, bf16[1,2,512,1024]{3,2,1,0:T(8,128)(2,1)S(1)} %copy-done.6), kind=kOutput, calls=%fused_computation.9 | convolution fusion | flops 1073741824 | bytes 5242880 | tf_op jit(solution)/shard_map/dot_general | solution.py:17
  13.8 3.6 %fusion.20 = bf16[1,512,1024]{2,1,0:T(8,128)(2,1)S(1)} fusion(f32[512,1024]{1,0:T(8,128)} %fusion.2, bf16[2,1024,1024]{2,1,0:T(8,128)(2,1)} %param.11, bf16[1,2,512,1024]{3,2,1,0:T(8,128)(2,1)S(1)} %copy-done.6), kind=kOutput, calls=%fused_computation.29 | convolution fusion | flops 1074790400 | bytes 6291456 | tf_op jit(solution)/shard_map/dot_general | solution.py:14
  17.4 0.0 copy-done.5
  17.4 0.5 copy-done.8
  17.9 1.3 fusion.23
  19.2 0.0 copy-start.3
  19.2 0.5 broadcast_select_fusion
  19.7 4.1 %collective-permute-start = (bf16[2,512,512]{2,1,0:T(8,128)(2,1)S(1)}, bf16[2,512,512]{2,1,0:T(8,128)(2,1)}, u32[]{:S(2)}, u32[]{:S(2)}) collective-permute-start(bf16[2,512,512]{2,1,0:T(8,128)(2,1)S(1)} %get-tuple-element.5), channel_id=1, source_target_pairs={{0,8},{2,10},{4,12},{6,14},{8,0},{10,2},{12,4},{14,6},{1,9},{3,11}... | collective-permute-start | bytes 3145736 | tf_op jit(solution)/shard_map/ppermute | solution.py:10
  23.8 0.0 copy-done.3
  23.8 4.5 %scatter_custom_fusion = s32[1024]{0:T(1024)S(1)} fusion(s32[1024]{0:T(1024)S(1)} %compare_select_fusion.1, s32[1024]{0:T(1024)S(1)} %iota.11, s32[]{:T(128)} %constant.69.clone.1), kind=kCustom, calls=%fused_computation.69 | custom fusion | bytes 4100 | tf_op jit(solution)/shard_map/scatter | solution.py:34
  28.3 27.6 %gather_fusion = bf16[1024,2,1024]{2,0,1:T(8,128)(2,1)} fusion(bf16[2,1024,1024]{2,1,0:T(8,128)(2,1)} %param.12, s32[1024]{0:T(1024)S(1)} %fusion.46), kind=kCustom, calls=%fused_computation | custom fusion | bytes 8392704 | tf_op jit(solution)/shard_map/jit(_take)/gather | solution.py:35
  56.0 2.6 %select_bitcast_fusion = bf16[2,1024,1024]{2,1,0:T(8,128)(2,1)S(1)} fusion(bf16[1024,2,1024]{2,0,1:T(8,128)(2,1)} %gather_fusion, pred[1024]{0:T(1024)(128)(4,1)S(1)} %compare_and_fusion), kind=kLoop, calls=%fused_computation.3 | loop fusion | flops 2097152 | bytes 8389632 | tf_op jit(solution)/shard_map/jit(_take)/select_n | solution.py:35
  58.6 10.9 %collective-permute-done = bf16[2,512,512]{2,1,0:T(8,128)(2,1)} collective-permute-done((bf16[2,512,512]{2,1,0:T(8,128)(2,1)S(1)}, bf16[2,512,512]{2,1,0:T(8,128)(2,1)}, u32[]{:S(2)}, u32[]{:S(2)}) %collective-permute-start) | collective-permute-done | bytes 1048608 | tf_op jit(solution)/shard_map/ppermute | solution.py:10
  69.6 2.2 %maximum_select_fusion = bf16[2,512,1024]{2,1,0:T(8,128)(2,1)S(1)} fusion(bf16[2,512,512]{2,1,0:T(8,128)(2,1)} %collective-permute-done, bf16[2,512,512]{2,1,0:T(8,128)(2,1)S(1)} %get-tuple-element.6, bf16[2,512,512]{2,1,0:T(8,128)(2,1)S(1)} %get-tuple-element.7, pred[]{:T(512)S(6)} %eq.15), kind=kLoop, calls=%fused_computation.8 | loop fusion | flops 9437184 | bytes 5242881 | tf_op jit(solution)/shard_map/jit(_where)/select_n | solution.py:43
  71.8 1.3 fusion.8
  73.1 1.3 fusion.11
  74.3 0.0 copy-start
  74.3 1.3 subtract_convert_fusion
  75.6 0.0 copy-done
  75.6 0.4 fusion.40
  76.1 0.5 fusion.36
  76.6 1.3 add_convert_fusion
  77.9 0.5 convolution_subtract_fusion
  78.3 0.5 convolution_add_fusion
  78.8 0.0 copy-start.7
  78.8 0.0 copy-start.2
  78.8 0.0 copy-start.1
  78.8 1.1 pad_maximum_fusion.1
  79.9 5.8 %all-to-all-start = ((f32[2,8,64,256]{3,2,0,1:T(8,128)}), f32[2,8,64,256]{3,2,0,1:T(8,128)S(1)}, u32[]{:S(2)}, u32[]{:S(2)}) async-start(f32[2,8,64,256]{3,2,0,1:T(8,128)} %pad_maximum_fusion.1), calls=%async_computation | async-start | bytes 2097152 | tf_op jit(solution)/shard_map/all_to_all | solution.py:50
  85.7 0.0 all-reduce.2.cloned.1.call-start
  85.7 0.0 copy-done.7
  85.7 0.6 fusion.52
  86.3 0.6 compare_convert_fusion
  86.9 0.0 copy-done.2
  86.9 0.0 copy-done.1
  87.0 0.1 multiply_reduce_fusion
  87.1 24.5 %all-to-all-done = f32[2,8,64,256]{3,2,0,1:T(8,128)S(1)} async-done(((f32[2,8,64,256]{3,2,0,1:T(8,128)}), f32[2,8,64,256]{3,2,0,1:T(8,128)S(1)}, u32[]{:S(2)}, u32[]{:S(2)}) %all-to-all-start) | async-done | bytes 1048608 | tf_op jit(solution)/shard_map/all_to_all | solution.py:50
  111.6 0.8 copy.17
  112.4 2.6 %gather_fusion.1 = f32[512,2,256]{2,1,0:T(2,128)S(1)} fusion(f32[2,512,256]{2,0,1:T(2,128)S(1)} %bitcast.83, s32[1024]{0:T(1024)S(1)} %pad_clamp_fusion), kind=kCustom, calls=%fused_computation.1 | custom fusion | bytes 2099200 | tf_op jit(solution)/shard_map/jit(_take)/gather | solution.py:57
  115.0 0.2 fusion.31
  115.2 0.1 multiply_subtract_fusion
  115.3 1.0 pad_maximum_fusion.2
  116.3 0.0 all-reduce.2.cloned.1.call-update
  116.3 18.6 %all-reduce.2.cloned.1.call-done = f32[2,512,256]{2,1,0:T(8,128)} async-done(((f32[2,512,256]{2,1,0:T(8,128)}), f32[2,512,256]{2,1,0:T(8,128)}) %all-reduce.2.cloned.1.call-update) | async-done | bytes 1048592 | tf_op jit(solution)/shard_map/psum | solution.py:64
  135.0 2.3 %copy.23 = f32[2,512,256]{2,1,0:T(8,128)} copy(f32[2,512,256]{2,1,0:T(8,128)} %all-reduce.2.cloned.1.call-done) | data formatting | bytes 2097152
  (12 shorter events, 0.0 us)
Async XLA Ops:
  6.5 4.6 %copy-start.4 = (bf16[2,1024,1024]{2,1,0:T(8,128)(2,1)S(1)}, bf16[2,1024,1024]{2,1,0:T(8,128)(2,1)}, u32[]{:S(2)}) copy-start(bf16[2,1024,1024]{2,1,0:T(8,128)(2,1)} %param.11) | copy-start | bytes 12582916
  6.5 4.6 %copy-start.6 = (bf16[1,2,512,1024]{3,2,1,0:T(8,128)(2,1)S(1)}, bf16[1,2,512,1024]{3,2,1,0:T(8,128)(2,1)}, u32[]{:S(2)}) copy-start(bf16[1,2,512,1024]{3,2,1,0:T(8,128)(2,1)} %param.8) | copy-start | bytes 6291460
  13.8 3.6 %copy-start.5 = (bf16[2,1024,1024]{2,1,0:T(8,128)(2,1)S(1)}, bf16[2,1024,1024]{2,1,0:T(8,128)(2,1)}, u32[]{:S(2)}) copy-start(bf16[2,1024,1024]{2,1,0:T(8,128)(2,1)} %param.11) | copy-start | bytes 12582916
  13.8 4.1 %copy-start.8 = (f32[512,1024]{1,0:T(8,128)S(1)}, f32[512,1024]{1,0:T(8,128)}, u32[]{:S(2)}) copy-start(f32[512,1024]{1,0:T(8,128)} %fusion) | copy-start | bytes 6291460
  19.2 4.6 %copy-start.3 = (s32[1024]{0:T(1024)S(1)}, s32[1024]{0:T(1024)}, u32[]{:S(2)}) copy-start(s32[1024]{0:T(1024)} %param.10) | copy-start | bytes 12292
  19.7 49.9 %collective-permute-start = (bf16[2,512,512]{2,1,0:T(8,128)(2,1)S(1)}, bf16[2,512,512]{2,1,0:T(8,128)(2,1)}, u32[]{:S(2)}, u32[]{:S(2)}) collective-permute-start(bf16[2,512,512]{2,1,0:T(8,128)(2,1)S(1)} %get-tuple-element.5), channel_id=1, source_target_pairs={{0,8},{2,10},{4,12},{6,14},{8,0},{10,2},{12,4},{14,6},{1,9},{3,11}... | collective-permute-start | bytes 3145736 | tf_op jit(solution)/shard_map/ppermute | solution.py:10
  74.3 1.3 copy-start
  78.8 6.9 %copy-start.7 = (s32[1,4]{1,0:T(1,128)S(1)}, s32[1,4]{1,0:T(1,128)}, u32[]{:S(2)}) copy-start(s32[1,4]{1,0:T(1,128)} %param.9) | copy-start | bytes 52
  78.8 8.1 %copy-start.2 = (s32[512]{0:T(512)S(1)}, s32[512]{0:T(512)}, u32[]{:S(2)}) copy-start(s32[512]{0:T(512)} %param.15) | copy-start | bytes 6148
  78.8 8.1 %copy-start.1 = (f32[16,2,256]{2,1,0:T(2,128)S(1)}, f32[16,2,256]{2,1,0:T(2,128)}, u32[]{:S(2)}) copy-start(f32[16,2,256]{2,1,0:T(2,128)} %param.14) | copy-start | bytes 98308
  79.9 31.7 %all-to-all-start = ((f32[2,8,64,256]{3,2,0,1:T(8,128)}), f32[2,8,64,256]{3,2,0,1:T(8,128)S(1)}, u32[]{:S(2)}, u32[]{:S(2)}) async-start(f32[2,8,64,256]{3,2,0,1:T(8,128)} %pad_maximum_fusion.1), calls=%async_computation | async-start | bytes 2097152 | tf_op jit(solution)/shard_map/all_to_all | solution.py:50
  85.7 49.3 %all-reduce.2.cloned.1.call-start = ((), (), s32[]{:S(2)}) async-start(), calls=%async_computation.1 | async-start | bytes 2097152 | tf_op jit(solution)/shard_map/psum | solution.py:64
Sparse Core Ops, SparseCore 0:
  116.5 18.4 all-reduce.1
where the time goes:
time: 145 us; the launch traced here: 144 us
  waiting for transfers between devices  54.1 us (37%)
  local copies, waits for them, and re-layouts  38.3 us (26%)
  matrix products  19.1 us (13%)
  between operations  13.7 us (9%)
  starting transfers between devices  9.93 us (7%)
  other arithmetic  9.01 us (6%)
    gather x1, local copies, waits for them, and re-layouts, on_device(): reordered = jnp.take(branch_second, inverse, axis=1)  27.6 us
    all_to_all x1, waiting for transfers between devices, on_device(): lax.all_to_all(contracted.reshape(2, stem_size, block_rows, contracted.sh...  24.5 us
    psum x1, waiting for transfers between devices, on_device(): return lax.psum(total, 'cuts')  18.6 us
    ppermute x1, waiting for transfers between devices, swapped(): return lax.ppermute(value, axis, pairs)  10.9 us
    dot_general x3, matrix products, complex_dot(): jnp.dot(operand[1], matrix[1], preferred_element_type=jnp.float32)  6.33 us
    all_to_all x1, starting transfers between devices, on_device(): lax.all_to_all(contracted.reshape(2, stem_size, block_rows, contracted.sh...  5.77 us
    dot_general x3, matrix products, complex_dot(): jnp.dot(operand[0], matrix[0], preferred_element_type=jnp.float32)  5.36 us
    scatter x1, local copies, waits for them, and re-layouts, on_device(): jnp.zeros_like(index_order).at[index_order]  4.49 us
  transfers between devices with their start and end apart: 3, of which 3 were waited for; matrix products, arithmetic and copies ran while one was open for 25% of the time, Pallas kernels for 0%

commit v1 on v0

--- a/solution.py
+++ b/solution.py
@@ -2,6 +2,29 @@
 import jax.numpy as jnp
 from jax import lax
 from jax.sharding import PartitionSpec as P
+
+
+def split_up(shard, dim, size):
+    before, after = (shard.shape[:dim], shard.shape[dim + 1 :])
+    return jnp.moveaxis(shard.reshape(*before, size, -1, *after), dim, 0)
+
+
+def laid_out(parts, dim):
+    parts = jnp.moveaxis(parts, 0, dim)
+    dims = parts.shape
+    return parts.reshape(*dims[:dim], dims[dim] * dims[dim + 1], *dims[dim + 2 :])
+
+
+def exchange_directly(x, axis, split_dim, concat_dim):
+    count, place = (lax.axis_size(axis), lax.axis_index(axis))
+    blocks = split_up(x, split_dim, count)
+    result = blocks
+    for lap in range(1, count):
+        target, source = ((place + lap) % count, (place - lap) % count)
+        sent = lax.dynamic_index_in_dim(blocks, target, 0)
+        other = lax.ppermute(sent, axis, [(i, (i + lap) % count) for i in range(count)])
+        result = lax.dynamic_update_slice_in_dim(result, other, source, axis=0)
+    return laid_out(result, concat_dim)
 
 
 def swapped(value, axis, distance):
@@ -47,12 +70,8 @@
     )
     second = complex_dot(joined, reordered).astype(jnp.bfloat16)
     contracted = complex_dot(second, branch_third)
-    moved = lax.all_to_all(
-        contracted.reshape(2, stem_size, block_rows, contracted.shape[2]),
-        "stem",
-        split_axis=1,
-        concat_axis=1,
-        tiled=True,
+    moved = exchange_directly(
+        contracted.reshape(2, stem_size, block_rows, contracted.shape[2]), "stem", 1, 1
     )
     third = jnp.take(moved.reshape(2, rows_dev, contracted.shape[2]), picks, axis=1)
     code = jnp.sum(edge_values[0] * powers)

time: 145 us -> 140 us (0.966)
  waiting for transfers between devices: 54.1 us -> 41.2 us
  starting transfers between devices: 9.93 us -> 18.2 us
    all_to_all x1 -> x0, waiting for transfers between devices: 24.5 us -> none  [on_device(): lax.all_to_all(contracted.reshape(2, stem_size, block_rows, contracted.sh...]
    ppermute x0 -> x7, starting transfers between devices: none -> 14.1 us  [exchange_directly(): lax.ppermute(sent, axis, [(i, (i + lap) % count) for i in range(count)])]
    ppermute x0 -> x7, waiting for transfers between devices: none -> 8.56 us  [exchange_directly(): lax.ppermute(sent, axis, [(i, (i + lap) % count) for i in range(count)])]
    all_to_all x1 -> x0, starting transfers between devices: 5.77 us -> none  [on_device(): lax.all_to_all(contracted.reshape(2, stem_size, block_rows, contracted.sh...]
    psum x1, waiting for transfers between devices: 18.6 us -> 23.5 us  [on_device(): return lax.psum(total, 'cuts')]
    ppermute x1, waiting for transfers between devices: 10.9 us -> 9.17 us  [swapped(): return lax.ppermute(value, axis, pairs)]
  transfers between devices with their start and end apart: 3 -> 9, of which waited for: 3 -> 6; matrix products, arithmetic and copies ran while one was open for 25% -> 26% of each run, Pallas kernels for 0% -> 0%
where the time goes in v1:
time: 140 us; the launch traced here: 139 us
  waiting for transfers between devices  41.2 us (29%)
  local copies, waits for them, and re-layouts  38.5 us (28%)
  matrix products  19 us (14%)
  starting transfers between devices  18.2 us (13%)
  between operations  14 us (10%)
  other arithmetic  8.09 us (6%)
    gather x1, local copies, waits for them, and re-layouts, on_device(): reordered = jnp.take(branch_second, inverse, axis=1)  27.7 us
    psum x1, waiting for transfers between devices, on_device(): return lax.psum(total, 'cuts')  23.5 us
    ppermute x7, starting transfers between devices, exchange_directly(): lax.ppermute(sent, axis, [(i, (i + lap) % count) for i in range(count)])  14.1 us
    ppermute x1, waiting for transfers between devices, swapped(): return lax.ppermute(value, axis, pairs)  9.17 us
    ppermute x7, waiting for transfers between devices, exchange_directly(): lax.ppermute(sent, axis, [(i, (i + lap) % count) for i in range(count)])  8.56 us
    dot_general x3, matrix products, complex_dot(): jnp.dot(operand[1], matrix[1], preferred_element_type=jnp.float32)  6.33 us
    dot_general x3, matrix products, complex_dot(): jnp.dot(operand[0], matrix[0], preferred_element_type=jnp.float32)  5.34 us
    scatter x1, local copies, waits for them, and re-layouts, on_device(): jnp.zeros_like(index_order).at[index_order]  4.49 us
  transfers between devices with their start and end apart: 9, of which 6 were waited for; matrix products, arithmetic and copies ran while one was open for 26% of the time, Pallas kernels for 0%

profile of v1, /device:TPU:0, one launch (start us, length us, event | category | flops | bytes accessed | tf_op | source)
XLA Modules:
  0.0 138.9 jit_solution(3341475410471258741)
XLA Ops:
  6.5 4.6 %fusion.2 = f32[512,1024]{1,0:T(8,128)} fusion(bf16[2,1024,1024]{2,1,0:T(8,128)(2,1)} %param.11, bf16[1,2,512,1024]{3,2,1,0:T(8,128)(2,1)} %param.8), kind=kOutput, calls=%fused_computation.26 | convolution fusion | flops 1073741824 | bytes 5242880 | tf_op jit(solution)/shard_map/dot_general | solution.py:37
  11.2 2.6 %fusion = f32[512,1024]{1,0:T(8,128)} fusion(bf16[2,1024,1024]{2,1,0:T(8,128)(2,1)S(1)} %copy-done.4, bf16[1,2,512,1024]{3,2,1,0:T(8,128)(2,1)S(1)} %copy-done.6), kind=kOutput, calls=%fused_computation.24 | convolution fusion | flops 1073741824 | bytes 5242880 | tf_op jit(solution)/shard_map/dot_general | solution.py:40
  13.7 3.6 %fusion.20 = bf16[1,512,1024]{2,1,0:T(8,128)(2,1)S(1)} fusion(f32[512,1024]{1,0:T(8,128)} %fusion.2, bf16[2,1024,1024]{2,1,0:T(8,128)(2,1)} %param.11, bf16[1,2,512,1024]{3,2,1,0:T(8,128)(2,1)S(1)} %copy-done.6), kind=kOutput, calls=%fused_computation.44 | convolution fusion | flops 1074790400 | bytes 6291456 | tf_op jit(solution)/shard_map/dot_general | solution.py:37
  17.4 0.5 copy-done.8
  17.9 1.3 fusion.23
  19.2 0.0 copy-start.2
  19.2 0.0 copy-start.3
  19.2 0.0 copy-start.7
  19.2 0.5 broadcast_select_fusion
  19.7 4.1 %collective-permute-start = (bf16[2,512,512]{2,1,0:T(8,128)(2,1)S(1)}, bf16[2,512,512]{2,1,0:T(8,128)(2,1)}, u32[]{:S(2)}, u32[]{:S(2)}) collective-permute-start(bf16[2,512,512]{2,1,0:T(8,128)(2,1)S(1)} %get-tuple-element.5), channel_id=1, source_target_pairs={{0,8},{2,10},{4,12},{6,14},{8,0},{10,2},{12,4},{14,6},{1,9},{3,11}... | collective-permute-start | bytes 3145736 | tf_op jit(solution)/shard_map/ppermute | solution.py:33
  23.8 4.5 %scatter_custom_fusion = s32[1024]{0:T(1024)S(1)} fusion(s32[1024]{0:T(1024)S(1)} %compare_select_fusion.1, s32[1024]{0:T(1024)S(1)} %iota.11, s32[]{:T(128)} %constant.156.clone.1), kind=kCustom, calls=%fused_computation.105 | custom fusion | bytes 4100 | tf_op jit(solution)/shard_map/scatter | solution.py:57
  28.4 0.6 fusion.67
  29.0 0.6 compare_convert_fusion
  29.9 0.0 copy-start.1
  29.9 27.7 %gather_fusion = bf16[1024,2,1024]{2,0,1:T(8,128)(2,1)} fusion(bf16[2,1024,1024]{2,1,0:T(8,128)(2,1)} %param.12, s32[1024]{0:T(1024)S(1)} %fusion.61), kind=kCustom, calls=%fused_computation | custom fusion | bytes 8392704 | tf_op jit(solution)/shard_map/jit(_take)/gather | solution.py:58
  57.6 0.1 multiply_reduce_fusion
  57.7 2.6 %select_bitcast_fusion = bf16[2,1024,1024]{2,1,0:T(8,128)(2,1)S(1)} fusion(bf16[1024,2,1024]{2,0,1:T(8,128)(2,1)} %gather_fusion, pred[1024]{0:T(1024)(128)(4,1)S(1)} %compare_and_fusion), kind=kLoop, calls=%fused_computation.3 | loop fusion | flops 2097152 | bytes 8389632 | tf_op jit(solution)/shard_map/jit(_take)/select_n | solution.py:58
  60.4 9.2 %collective-permute-done = bf16[2,512,512]{2,1,0:T(8,128)(2,1)} collective-permute-done((bf16[2,512,512]{2,1,0:T(8,128)(2,1)S(1)}, bf16[2,512,512]{2,1,0:T(8,128)(2,1)}, u32[]{:S(2)}, u32[]{:S(2)}) %collective-permute-start) | collective-permute-done | bytes 1048608 | tf_op jit(solution)/shard_map/ppermute | solution.py:33
  69.5 2.1 %maximum_select_fusion = bf16[2,512,1024]{2,1,0:T(8,128)(2,1)S(1)} fusion(bf16[2,512,512]{2,1,0:T(8,128)(2,1)} %collective-permute-done, bf16[2,512,512]{2,1,0:T(8,128)(2,1)S(1)} %get-tuple-element.6, bf16[2,512,512]{2,1,0:T(8,128)(2,1)S(1)} %get-tuple-element.7, pred[]{:T(512)S(6)} %eq.29), kind=kLoop, calls=%fused_computation.23 | loop fusion | flops 9437184 | bytes 5242881 | tf_op jit(solution)/shard_map/jit(_where)/select_n | solution.py:66
  71.7 1.3 fusion.8
  72.9 1.3 fusion.11
  74.2 1.3 subtract_convert_fusion
  75.5 0.4 fusion.41
  76.0 0.4 fusion.37
  76.4 1.3 add_convert_fusion
  77.7 0.5 convolution_subtract_fusion
  78.2 0.5 convolution_add_fusion
  78.6 0.1 fusion.60
  78.7 1.6 %collective-permute-start.1 = (f32[1,2,1,64,256]{4,3,0,2,1:T(8,128)S(1)}, f32[1,2,1,64,256]{4,3,0,2,1:T(8,128)S(1)}, u32[]{:S(2)}, u32[]{:S(2)}) collective-permute-start(f32[1,2,1,64,256]{4,3,0,2,1:T(8,128)S(1)} %get-tuple-element.11), channel_id=1, source_target_pairs={{0,2},{2,4},{4,6},{6,8},{8,10},{10,12},{12,14},{14,0},{1,3},{3,5},... | collective-permute-start | bytes 393224 | tf_op jit(solution)/shard_map/ppermute | solution.py:25
  80.3 0.1 fusion.27
  80.4 0.6 collective-permute-start.2
  81.0 3.3 %collective-permute-start.6 = (f32[1,2,1,64,256]{4,3,0,2,1:T(8,128)S(1)}, f32[1,2,1,64,256]{4,3,0,2,1:T(8,128)S(1)}, u32[]{:S(2)}, u32[]{:S(2)}) collective-permute-start(f32[1,2,1,64,256]{4,3,0,2,1:T(8,128)S(1)} %fusion.58), channel_id=1, source_target_pairs={{0,12},{2,14},{4,0},{6,2},{8,4},{10,6},{12,8},{14,10},{1,13},{3,15... | collective-permute-start | bytes 393224 | tf_op jit(solution)/shard_map/ppermute | solution.py:25
  84.3 0.2 collective-permute-start.3
  84.6 1.7 %collective-permute-start.4 = (f32[1,2,1,64,256]{4,3,0,2,1:T(8,128)S(1)}, f32[1,2,1,64,256]{4,3,0,2,1:T(8,128)S(1)}, u32[]{:S(2)}, u32[]{:S(2)}) collective-permute-start(f32[1,2,1,64,256]{4,3,0,2,1:T(8,128)S(1)} %get-tuple-element.14), channel_id=1, source_target_pairs={{0,8},{2,10},{4,12},{6,14},{8,0},{10,2},{12,4},{14,6},{1,9},{3,11}... | collective-permute-start | bytes 393224 | tf_op jit(solution)/shard_map/ppermute | solution.py:25
  86.3 1.6 %collective-permute-done.1 = f32[1,2,1,64,256]{4,3,0,2,1:T(8,128)S(1)} collective-permute-done((f32[1,2,1,64,256]{4,3,0,2,1:T(8,128)S(1)}, f32[1,2,1,64,256]{4,3,0,2,1:T(8,128)S(1)}, u32[]{:S(2)}, u32[]{:S(2)}) %collective-permute-start.1) | collective-permute-done | bytes 131104 | tf_op jit(solution)/shard_map/ppermute | solution.py:25
  87.9 0.6 collective-permute-start.5
  88.5 0.1 collective-permute-done.2
  88.6 6.1 %collective-permute-start.7 = (f32[1,2,1,64,256]{4,3,0,2,1:T(8,128)S(1)}, f32[1,2,1,64,256]{4,3,0,2,1:T(8,128)S(1)}, u32[]{:S(2)}, u32[]{:S(2)}) collective-permute-start(f32[1,2,1,64,256]{4,3,0,2,1:T(8,128)S(1)} %get-tuple-element.10), channel_id=1, source_target_pairs={{0,14},{2,0},{4,2},{6,4},{8,6},{10,8},{12,10},{14,12},{1,15},{3,1}... | collective-permute-start | bytes 393224 | tf_op jit(solution)/shard_map/ppermute | solution.py:25
  94.7 6.4 %collective-permute-done.3 = f32[1,2,1,64,256]{4,3,0,2,1:T(8,128)S(1)} collective-permute-done((f32[1,2,1,64,256]{4,3,0,2,1:T(8,128)S(1)}, f32[1,2,1,64,256]{4,3,0,2,1:T(8,128)S(1)}, u32[]{:S(2)}, u32[]{:S(2)}) %collective-permute-start.3) | collective-permute-done | bytes 131104 | tf_op jit(solution)/shard_map/ppermute | solution.py:25
  101.1 0.4 collective-permute-done.4
  101.6 0.8 copy.11
  102.4 2.6 %gather_fusion.1 = f32[512,2,256]{2,1,0:T(2,128)S(1)} fusion(f32[2,512,256]{2,0,1:T(2,128)S(1)} %bitcast.102, s32[1024]{0:T(1024)S(1)} %pad_clamp_fusion), kind=kCustom, calls=%fused_computation.1 | custom fusion | bytes 2099200 | tf_op jit(solution)/shard_map/jit(_take)/gather | solution.py:76
  105.0 0.2 fusion.32
  105.2 0.1 multiply_subtract_fusion
  105.3 1.0 pad_maximum_fusion.2
  106.3 0.0 all-reduce.2.cloned.1.call-update
  106.3 23.5 %all-reduce.2.cloned.1.call-done = f32[2,512,256]{2,1,0:T(8,128)} async-done(((f32[2,512,256]{2,1,0:T(8,128)}), f32[2,512,256]{2,1,0:T(8,128)}) %all-reduce.2.cloned.1.call-update) | async-done | bytes 1048592 | tf_op jit(solution)/shard_map/psum | solution.py:83
  129.8 2.3 %copy.24 = f32[2,512,256]{2,1,0:T(8,128)} copy(f32[2,512,256]{2,1,0:T(8,128)} %all-reduce.2.cloned.1.call-done) | data formatting | bytes 2097152
  (33 shorter events, 0.2 us)
Async XLA Ops:
  6.5 123.3 %all-reduce.2.cloned.1.call-start = ((), (), s32[]{:S(2)}) async-start(), calls=%async_computation | async-start | bytes 2097152 | tf_op jit(solution)/shard_map/psum | solution.py:83
  6.5 4.6 %copy-start.4 = (bf16[2,1024,1024]{2,1,0:T(8,128)(2,1)S(1)}, bf16[2,1024,1024]{2,1,0:T(8,128)(2,1)}, u32[]{:S(2)}) copy-start(bf16[2,1024,1024]{2,1,0:T(8,128)(2,1)} %param.11) | copy-start | bytes 12582916
  6.5 4.6 %copy-start.6 = (bf16[1,2,512,1024]{3,2,1,0:T(8,128)(2,1)S(1)}, bf16[1,2,512,1024]{3,2,1,0:T(8,128)(2,1)}, u32[]{:S(2)}) copy-start(bf16[1,2,512,1024]{3,2,1,0:T(8,128)(2,1)} %param.8) | copy-start | bytes 6291460
  13.7 3.6 %copy-start.5 = (bf16[2,1024,1024]{2,1,0:T(8,128)(2,1)S(1)}, bf16[2,1024,1024]{2,1,0:T(8,128)(2,1)}, u32[]{:S(2)}) copy-start(bf16[2,1024,1024]{2,1,0:T(8,128)(2,1)} %param.11) | copy-start | bytes 12582916
  13.7 4.1 %copy-start.8 = (f32[512,1024]{1,0:T(8,128)S(1)}, f32[512,1024]{1,0:T(8,128)}, u32[]{:S(2)}) copy-start(f32[512,1024]{1,0:T(8,128)} %fusion) | copy-start | bytes 6291460
  19.2 4.6 %copy-start.2 = (s32[512]{0:T(512)S(1)}, s32[512]{0:T(512)}, u32[]{:S(2)}) copy-start(s32[512]{0:T(512)} %param.15) | copy-start | bytes 6148
  19.2 4.6 %copy-start.3 = (s32[1024]{0:T(1024)S(1)}, s32[1024]{0:T(1024)}, u32[]{:S(2)}) copy-start(s32[1024]{0:T(1024)} %param.10) | copy-start | bytes 12292
  19.2 9.2 %copy-start.7 = (s32[1,4]{1,0:T(1,128)S(1)}, s32[1,4]{1,0:T(1,128)}, u32[]{:S(2)}) copy-start(s32[1,4]{1,0:T(1,128)} %param.9) | copy-start | bytes 52
  19.7 49.9 %collective-permute-start = (bf16[2,512,512]{2,1,0:T(8,128)(2,1)S(1)}, bf16[2,512,512]{2,1,0:T(8,128)(2,1)}, u32[]{:S(2)}, u32[]{:S(2)}) collective-permute-start(bf16[2,512,512]{2,1,0:T(8,128)(2,1)S(1)} %get-tuple-element.5), channel_id=1, source_target_pairs={{0,8},{2,10},{4,12},{6,14},{8,0},{10,2},{12,4},{14,6},{1,9},{3,11}... | collective-permute-start | bytes 3145736 | tf_op jit(solution)/shard_map/ppermute | solution.py:33
  29.9 27.7 %copy-start.1 = (f32[16,2,256]{2,1,0:T(2,128)S(1)}, f32[16,2,256]{2,1,0:T(2,128)}, u32[]{:S(2)}) copy-start(f32[16,2,256]{2,1,0:T(2,128)} %param.14) | copy-start | bytes 98308
  74.2 1.3 copy-start
  78.7 9.2 %collective-permute-start.1 = (f32[1,2,1,64,256]{4,3,0,2,1:T(8,128)S(1)}, f32[1,2,1,64,256]{4,3,0,2,1:T(8,128)S(1)}, u32[]{:S(2)}, u32[]{:S(2)}) collective-permute-start(f32[1,2,1,64,256]{4,3,0,2,1:T(8,128)S(1)} %get-tuple-element.11), channel_id=1, source_target_pairs={{0,2},{2,4},{4,6},{6,8},{8,10},{10,12},{12,14},{14,0},{1,3},{3,5},... | collective-permute-start | bytes 393224 | tf_op jit(solution)/shard_map/ppermute | solution.py:25
  80.4 8.2 %collective-permute-start.2 = (f32[1,2,1,64,256]{4,3,0,2,1:T(8,128)S(1)}, f32[1,2,1,64,256]{4,3,0,2,1:T(8,128)S(1)}, u32[]{:S(2)}, u32[]{:S(2)}) collective-permute-start(f32[1,2,1,64,256]{4,3,0,2,1:T(8,128)S(1)} %get-tuple-element.12), channel_id=1, source_target_pairs={{0,4},{2,6},{4,8},{6,10},{8,12},{10,14},{12,0},{14,2},{1,5},{3,7},... | collective-permute-start | bytes 393224 | tf_op jit(solution)/shard_map/ppermute | solution.py:25
  81.0 20.5 %collective-permute-start.6 = (f32[1,2,1,64,256]{4,3,0,2,1:T(8,128)S(1)}, f32[1,2,1,64,256]{4,3,0,2,1:T(8,128)S(1)}, u32[]{:S(2)}, u32[]{:S(2)}) collective-permute-start(f32[1,2,1,64,256]{4,3,0,2,1:T(8,128)S(1)} %fusion.58), channel_id=1, source_target_pairs={{0,12},{2,14},{4,0},{6,2},{8,4},{10,6},{12,8},{14,10},{1,13},{3,15... | collective-permute-start | bytes 393224 | tf_op jit(solution)/shard_map/ppermute | solution.py:25
  84.3 16.7 %collective-permute-start.3 = (f32[1,2,1,64,256]{4,3,0,2,1:T(8,128)S(1)}, f32[1,2,1,64,256]{4,3,0,2,1:T(8,128)S(1)}, u32[]{:S(2)}, u32[]{:S(2)}) collective-permute-start(f32[1,2,1,64,256]{4,3,0,2,1:T(8,128)S(1)} %get-tuple-element.13), channel_id=1, source_target_pairs={{0,6},{2,8},{4,10},{6,12},{8,14},{10,0},{12,2},{14,4},{1,7},{3,9},... | collective-permute-start | bytes 393224 | tf_op jit(solution)/shard_map/ppermute | solution.py:25
  84.6 16.9 %collective-permute-start.4 = (f32[1,2,1,64,256]{4,3,0,2,1:T(8,128)S(1)}, f32[1,2,1,64,256]{4,3,0,2,1:T(8,128)S(1)}, u32[]{:S(2)}, u32[]{:S(2)}) collective-permute-start(f32[1,2,1,64,256]{4,3,0,2,1:T(8,128)S(1)} %get-tuple-element.14), channel_id=1, source_target_pairs={{0,8},{2,10},{4,12},{6,14},{8,0},{10,2},{12,4},{14,6},{1,9},{3,11}... | collective-permute-start | bytes 393224 | tf_op jit(solution)/shard_map/ppermute | solution.py:25
  87.9 13.6 %collective-permute-start.5 = (f32[1,2,1,64,256]{4,3,0,2,1:T(8,128)S(1)}, f32[1,2,1,64,256]{4,3,0,2,1:T(8,128)S(1)}, u32[]{:S(2)}, u32[]{:S(2)}) collective-permute-start(f32[1,2,1,64,256]{4,3,0,2,1:T(8,128)S(1)} %get-tuple-element.15), channel_id=1, source_target_pairs={{0,10},{2,12},{4,14},{6,0},{8,2},{10,4},{12,6},{14,8},{1,11},{3,13... | collective-permute-start | bytes 393224 | tf_op jit(solution)/shard_map/ppermute | solution.py:25
  88.6 12.9 %collective-permute-start.7 = (f32[1,2,1,64,256]{4,3,0,2,1:T(8,128)S(1)}, f32[1,2,1,64,256]{4,3,0,2,1:T(8,128)S(1)}, u32[]{:S(2)}, u32[]{:S(2)}) collective-permute-start(f32[1,2,1,64,256]{4,3,0,2,1:T(8,128)S(1)} %get-tuple-element.10), channel_id=1, source_target_pairs={{0,14},{2,0},{4,2},{6,4},{8,6},{10,8},{12,10},{14,12},{1,15},{3,1}... | collective-permute-start | bytes 393224 | tf_op jit(solution)/shard_map/ppermute | solution.py:25
Sparse Core Ops, SparseCore 0:
  106.5 23.3 all-reduce.1
